TPU v7x, 512 devices: a whole 4x8x8 slice. The times are simulated.
512 devices in a mesh: section: 16 (over y_lo, x, core), dp: 32 (over z, y_hi).
Axes of the slice: x: 4, y: 8 (y_hi: 4, y_lo: 2; y = y_hi * 2 + y_lo), z: 8, core: 2. Of those that a mesh axis runs over, the one named last changes fastest.
Arguments:
- stash: bfloat16 [16, 4096, 2048], P('section', 'dp'), may hold values from -6 to 6
- cotangent: bfloat16 [4096, 2048], P('dp', 'section'), may hold values from -6 to 6
- gate_weight: bfloat16 [16, 2048, 512], P('section', 'dp'), may hold values from -0.125 to 0.125
- up_weight: bfloat16 [16, 2048, 512], P('section', 'dp'), may hold values from -0.125 to 0.125
- down_weight: bfloat16 [16, 512, 2048], P('section'), may hold values from -0.25 to 0.25
- shared_gate: bfloat16 [16, 2048], P('section'), may hold values from -0.125 to 0.125
Outputs:
- grad_inputs: bfloat16 [16, 4096, 2048], P('section', 'dp')
- down_grad: float32 [16, 512, 2048], P('section', 'dp')
All inputs are finite; a program needn't handle non-finite values.
Results may differ from a plain program's by a relative error of at most 0.029.
Values may be sent and summed in bfloat16 or wider, within the bound.
A program may use at most 64 MiB of HBM per device.

v0:
```python
import jax
import jax.numpy as jnp
from jax import lax
from jax.sharding import PartitionSpec as P

ROWS = 64
MICRO = 2


def shifted(x, axis, by):
    size = lax.axis_size(axis)
    pairs = [(i, i + by) for i in range(size) if 0 <= i + by < size]
    return lax.ppermute(x, axis, pairs)


def chain_rows(grad_rows, projected, gate_score, hidden, joined, down_full, gate_vector):
    hidden_units = down_full.shape[0]
    gate_pre = projected[:, :hidden_units]
    up_pre = projected[:, hidden_units:]
    gate_sig = jax.nn.sigmoid(gate_pre)
    activated = gate_pre * gate_sig
    back_proj = lax.dot_general(
        grad_rows, down_full, (((1,), (1,)), ((), ())), preferred_element_type=jnp.float32
    )
    gate_sum = jnp.sum(back_proj * hidden.astype(jnp.float32), axis=1, keepdims=True)
    hidden_grad = gate_score * back_proj
    gate_grad = hidden_grad * up_pre * gate_sig * (1.0 + gate_pre * (1.0 - gate_sig))
    up_grad = hidden_grad * activated
    pair_grad = jnp.concatenate([gate_grad, up_grad], axis=1).astype(jnp.bfloat16)
    through = lax.dot_general(
        pair_grad, joined, (((1,), (1,)), ((), ())), preferred_element_type=jnp.float32
    )
    logit_grad = gate_sum * gate_score * (1.0 - gate_score)
    return (
        grad_rows.astype(jnp.float32)
        + through
        + logit_grad * gate_vector.astype(jnp.float32)[None, :]
    ).astype(jnp.bfloat16)


def on_device(stash, cotangent, gate_weight, up_weight, down_weight, shared_gate):
    sections = lax.axis_size("section")
    replicas = lax.axis_size("dp")
    section_index = lax.axis_index("section")
    local_rows = stash.shape[1]
    model_width = stash.shape[2]
    own_rows = stash[0]
    blocks = own_rows.reshape(sections, local_rows // sections * model_width)
    blocks = lax.all_to_all(blocks, "section", split_axis=0, concat_axis=0, tiled=True)
    blocks = jnp.flip(blocks, 0)
    blocks = lax.all_to_all(blocks, "section", split_axis=0, concat_axis=0, tiled=True)
    own_rows = blocks.reshape(local_rows, model_width)
    seeded = lax.all_gather(cotangent, "section", axis=1, tiled=True)
    gate_full, up_full = (
        lax.all_gather(gate_weight[0], "dp", axis=0, tiled=True),
        lax.all_gather(up_weight[0], "dp", axis=0, tiled=True),
    )
    joined = jnp.concatenate([gate_full, up_full], axis=1)
    down_full = down_weight[0]
    gate_vector = shared_gate[0]
    hidden_units = down_full.shape[0]
    projected_all = jnp.dot(own_rows, joined, preferred_element_type=jnp.float32)
    score_all = jax.nn.sigmoid(jnp.dot(own_rows, gate_vector, preferred_element_type=jnp.float32))[
        :, None
    ]
    gate_all = projected_all[:, :hidden_units]
    hidden_all = (gate_all * jax.nn.sigmoid(gate_all) * projected_all[:, hidden_units:]).astype(
        jnp.bfloat16
    )
    tick_count = sections + MICRO - 1
    is_last = section_index == sections - 1
    offset = sections - 1 - section_index

    def advance(tick_now, received):
        micro_index = tick_now - offset
        active = jnp.logical_and(micro_index >= 0, micro_index < MICRO)
        row_start = jnp.clip(micro_index, 0, MICRO - 1) * ROWS
        seed_rows = lax.dynamic_slice_in_dim(seeded, row_start, ROWS, 0)
        grad_rows = jnp.where(is_last, seed_rows, received)
        pieces = (
            grad_rows,
            lax.dynamic_slice_in_dim(projected_all, row_start, ROWS, 0),
            lax.dynamic_slice_in_dim(score_all, row_start, ROWS, 0),
            lax.dynamic_slice_in_dim(hidden_all, row_start, ROWS, 0),
        )

        def compute(operands):
            return chain_rows(
                operands[0], operands[1], operands[2], operands[3], joined, down_full, gate_vector
            )

        def skip_step(operands):
            return jnp.zeros_like(operands[0])

        return (lax.cond(active, compute, skip_step, pieces), grad_rows)

    def one_tick(received, tick_now):
        outgoing, grad_rows = advance(tick_now, received)
        passed = shifted(outgoing, "section", -1)
        return (passed, (outgoing, grad_rows))

    start_rows = jnp.zeros((ROWS, model_width), jnp.bfloat16)
    received, (outs_seen, grads_seen) = lax.scan(
        one_tick, start_rows, jnp.arange(tick_count - 1, dtype=jnp.int32)
    )
    last_out, last_grad = advance(tick_count - 1, received)
    outs_seen = jnp.concatenate([outs_seen, last_out[None]], axis=0)
    grads_seen = jnp.concatenate([grads_seen, last_grad[None]], axis=0)
    results = lax.dynamic_slice_in_dim(outs_seen, offset, MICRO, 0).reshape(local_rows, model_width)
    grad_all = lax.dynamic_slice_in_dim(grads_seen, offset, MICRO, 0).reshape(
        local_rows, model_width
    )
    scaled_all = (score_all * grad_all.astype(jnp.float32)).astype(jnp.bfloat16)
    norm_factor = (local_rows * replicas) ** (-0.5)
    weight_part = lax.dot_general(
        hidden_all, scaled_all, (((0,), (0,)), ((), ())), preferred_element_type=jnp.float32
    )
    summed = lax.psum_scatter(
        weight_part.astype(jnp.bfloat16), "dp", scatter_dimension=0, tiled=True
    ).astype(jnp.float32)
    return (results[None], (summed * norm_factor)[None])


def solution(mesh):
    placed = (
        P("section", "dp", None),
        P("dp", "section"),
        P("section", "dp", None),
        P("section", "dp", None),
        P("section", None, None),
        P("section", None),
    )
    return jax.shard_map(
        on_device,
        mesh=mesh,
        in_specs=placed,
        out_specs=(P("section", "dp", None), P("section", "dp", None)),
        check_vma=False,
    )
```

profile of v0, /device:TPU:6, one launch (start us, length us, event | category | flops | bytes accessed | tf_op | source)
XLA Modules:
  0.0 667.4 jit_solution(10327479615474628272)
XLA Ops:
  11.6 3.8 reduce.2
  15.8 16.9 %all_to_all.22 = bf16[16,2,8192]{2,1,0:T(2,128)(2,1)S(1)} all-to-all(bf16[16,2,8192]{2,1,0:T(2,128)(2,1)S(1)} %reshape.37), channel_id=1, replica_groups=mesh['section'=16,'dp'=32] {'section'}, dimensions={0} | all-to-all | bytes 1048576 | tf_op jit(solution)/shard_map/all_to_all | solution.py:49
  38.5 5.8 all-to-all-start.1
  44.4 21.8 %all_gather.9 = bf16[128,2048]{1,0:T(8,128)(2,1)} all-gather(bf16[128,128]{1,0:T(8,128)(2,1)S(1)} %copy-done.3), channel_id=1, replica_groups=mesh['section'=16,'dp'=32] {'section'}, dimensions={1}, use_global_device_ids=true | all-gather | bytes 557056 | tf_op jit(solution)/shard_map/all_gather | solution.py:53
  70.4 31.4 %all-gather.5.cloned.1.call-done = bf16[1,2048,512]{2,1,0:T(8,128)(2,1)} async-done(((bf16[1,64,512]{2,1,0:T(8,128)(2,1)}), bf16[1,2048,512]{2,1,0:T(8,128)(2,1)}) %all-gather.5.cloned.1.call-update) | async-done | bytes 2097168 | tf_op jit(solution)/shard_map/all_gather | solution.py:55
  101.8 85.6 %all-gather.7.cloned.1.call-done = bf16[1,2048,512]{2,1,0:T(8,128)(2,1)} async-done(((bf16[1,64,512]{2,1,0:T(8,128)(2,1)}), bf16[1,2048,512]{2,1,0:T(8,128)(2,1)}) %all-gather.7.cloned.1.call-update) | async-done | bytes 2097168 | tf_op jit(solution)/shard_map/all_gather | solution.py:56
  193.3 229.1 %while.14 = (s32[]{:T(128)}, bf16[64,2048]{1,0:T(8,128)(2,1)S(1)}, bf16[16,64,2048]{2,1,0:T(8,128)(2,1)}, bf16[16,64,2048]{2,1,0:T(8,128)(2,1)}, s32[16]{0:T(128...) while((s32[]{:T(128)}, bf16[64,2048]{1,0:T(8,128)(2,1)S(1)}, ...), condition=%wide.region_4.5_spmd, body=%wide.region_0.4_spmd.sunk | while | flops 404260992 | bytes 10837449 | solution.py:103
  199.7 3.5 collective-permute-done
  206.9 3.7 collective-permute-start
  218.6 3.7 collective-permute-start
  230.3 3.7 collective-permute-start
  234.7 4.7 collective-permute-done
  246.3 6.8 %collective-permute-done = bf16[64,2048]{1,0:T(8,128)(2,1)S(1)} collective-permute-done((bf16[64,2048]{1,0:T(8,128)(2,1)}, bf16[64,2048]{1,0:T(8,128)(2,1)S(1)}, u32[]{:S(2)}, u32[]{:S(2)}) %collective-permute-start) | collective-permute-done | bytes 262176 | tf_op jit(solution)/shard_map/while/body/eval_jaxpr/ppermute | solution.py:13
  259.5 7.4 %collective-permute-done = bf16[64,2048]{1,0:T(8,128)(2,1)S(1)} collective-permute-done((bf16[64,2048]{1,0:T(8,128)(2,1)}, bf16[64,2048]{1,0:T(8,128)(2,1)S(1)}, u32[]{:S(2)}, u32[]{:S(2)}) %collective-permute-start) | collective-permute-done | bytes 262176 | tf_op jit(solution)/shard_map/while/body/eval_jaxpr/ppermute | solution.py:13
  273.2 7.4 %collective-permute-done = bf16[64,2048]{1,0:T(8,128)(2,1)S(1)} collective-permute-done((bf16[64,2048]{1,0:T(8,128)(2,1)}, bf16[64,2048]{1,0:T(8,128)(2,1)S(1)}, u32[]{:S(2)}, u32[]{:S(2)}) %collective-permute-start) | collective-permute-done | bytes 262176 | tf_op jit(solution)/shard_map/while/body/eval_jaxpr/ppermute | solution.py:13
  287.0 7.4 %collective-permute-done = bf16[64,2048]{1,0:T(8,128)(2,1)S(1)} collective-permute-done((bf16[64,2048]{1,0:T(8,128)(2,1)}, bf16[64,2048]{1,0:T(8,128)(2,1)S(1)}, u32[]{:S(2)}, u32[]{:S(2)}) %collective-permute-start) | collective-permute-done | bytes 262176 | tf_op jit(solution)/shard_map/while/body/eval_jaxpr/ppermute | solution.py:13
  300.7 20.0 %collective-permute-done = bf16[64,2048]{1,0:T(8,128)(2,1)S(1)} collective-permute-done((bf16[64,2048]{1,0:T(8,128)(2,1)}, bf16[64,2048]{1,0:T(8,128)(2,1)S(1)}, u32[]{:S(2)}, u32[]{:S(2)}) %collective-permute-start) | collective-permute-done | bytes 262176 | tf_op jit(solution)/shard_map/while/body/eval_jaxpr/ppermute | solution.py:13
  323.7 6.3 conditional.4
  324.7 4.3 fusion.1
  332.6 7.3 %collective-permute-done = bf16[64,2048]{1,0:T(8,128)(2,1)S(1)} collective-permute-done((bf16[64,2048]{1,0:T(8,128)(2,1)}, bf16[64,2048]{1,0:T(8,128)(2,1)S(1)}, u32[]{:S(2)}, u32[]{:S(2)}) %collective-permute-start) | collective-permute-done | bytes 262176 | tf_op jit(solution)/shard_map/while/body/eval_jaxpr/ppermute | solution.py:13
  342.9 6.3 conditional.4
  344.0 4.3 fusion.1
  351.9 3.5 collective-permute-done
  359.1 9.2 %collective-permute-start = (bf16[64,2048]{1,0:T(8,128)(2,1)}, bf16[64,2048]{1,0:T(8,128)(2,1)S(1)}, u32[]{:S(2)}, u32[]{:S(2)}) collective-permute-start(bf16[64,2048]{1,0:T(8,128)(2,1)} %get-tuple-element.350), channel_id=1, source_target_pairs={{32,0},{64,32},{96,64},{128,96},{160,128},{192,160},{224,192},{256... | collective-permute-start | bytes 786440 | tf_op jit(solution)/shard_map/while/body/eval_jaxpr/ppermute | solution.py:13
  376.2 3.7 collective-permute-start
  380.7 3.5 collective-permute-done
  387.9 3.7 collective-permute-start
  392.3 3.5 collective-permute-done
  399.5 3.7 collective-permute-start
  403.9 4.8 collective-permute-done
  416.0 6.4 collective-permute-done
  428.9 230.4 %reduce-scatter.2.cloned.1.call-done = bf16[16,2048]{1,0:T(8,128)(2,1)} async-done(((bf16[512,2048]{1,0:T(8,128)(2,1)}), bf16[16,2048]{1,0:T(8,128)(2,1)}) %reduce-scatter.2.cloned.1.call-update) | async-done | bytes 65552 | tf_op jit(solution)/shard_map/reduce_scatter | solution.py:118
  (155 shorter events, 131.2 us)
Async XLA Ops:
  7.2 94.6 %all-gather.5.cloned.1.call-start = ((), (), s32[]{:S(2)}) async-start(), calls=%async_computation.4 | async-start | bytes 2162688 | tf_op jit(solution)/shard_map/all_gather | solution.py:55
  7.9 179.5 %all-gather.7.cloned.1.call-start = ((), (), s32[]{:S(2)}) async-start(), calls=%async_computation.5 | async-start | bytes 2162688 | tf_op jit(solution)/shard_map/all_gather | solution.py:56
  15.8 28.6 %copy-start.2 = (bf16[1,2048]{1,0:T(2,128)(2,1)S(1)}, bf16[1,2048]{1,0:T(2,128)(2,1)}, u32[]{:S(2)}) copy-start(bf16[1,2048]{1,0:T(2,128)(2,1)} %param.17) | copy-start | bytes 12292
  15.8 28.6 %copy-start.3 = (bf16[128,128]{1,0:T(8,128)(2,1)S(1)}, bf16[128,128]{1,0:T(8,128)(2,1)}, u32[]{:S(2)}) copy-start(bf16[128,128]{1,0:T(8,128)(2,1)} %param.13) | copy-start | bytes 98308
  38.5 27.7 %all-to-all-start.1 = ((bf16[16,2,8192]{2,1,0:T(2,128)(2,1)}), bf16[16,2,8192]{2,1,0:T(2,128)(2,1)S(1)}, u32[]{:S(2)}, u32[]{:S(2)}) async-start(bf16[16,2,8192]{2,1,0:T(2,128)(2,1)} %reshape.39), calls=%async_computation.1 | async-start | bytes 1048576 | tf_op jit(solution)/shard_map/all_to_all | solution.py:51
  44.3 615.1 %reduce-scatter.2.cloned.1.call-start = ((), (), s32[]{:S(2)}) async-start(), calls=%async_computation.3 | async-start | bytes 2162688 | tf_op jit(solution)/shard_map/reduce_scatter | solution.py:118
  190.2 2.1 copy-start
  190.2 3.1 copy-start.1
  197.1 6.1 collective-permute-start
  206.9 7.9 %collective-permute-start = (bf16[64,2048]{1,0:T(8,128)(2,1)}, bf16[64,2048]{1,0:T(8,128)(2,1)S(1)}, u32[]{:S(2)}, u32[]{:S(2)}) collective-permute-start(bf16[64,2048]{1,0:T(8,128)(2,1)} %get-tuple-element.350), channel_id=1, source_target_pairs={{32,0},{64,32},{96,64},{128,96},{160,128},{192,160},{224,192},{256... | collective-permute-start | bytes 786440 | tf_op jit(solution)/shard_map/while/body/eval_jaxpr/ppermute | solution.py:13
  218.6 7.9 %collective-permute-start = (bf16[64,2048]{1,0:T(8,128)(2,1)}, bf16[64,2048]{1,0:T(8,128)(2,1)S(1)}, u32[]{:S(2)}, u32[]{:S(2)}) collective-permute-start(bf16[64,2048]{1,0:T(8,128)(2,1)} %get-tuple-element.350), channel_id=1, source_target_pairs={{32,0},{64,32},{96,64},{128,96},{160,128},{192,160},{224,192},{256... | collective-permute-start | bytes 786440 | tf_op jit(solution)/shard_map/while/body/eval_jaxpr/ppermute | solution.py:13
  230.3 9.1 %collective-permute-start = (bf16[64,2048]{1,0:T(8,128)(2,1)}, bf16[64,2048]{1,0:T(8,128)(2,1)S(1)}, u32[]{:S(2)}, u32[]{:S(2)}) collective-permute-start(bf16[64,2048]{1,0:T(8,128)(2,1)} %get-tuple-element.350), channel_id=1, source_target_pairs={{32,0},{64,32},{96,64},{128,96},{160,128},{192,160},{224,192},{256... | collective-permute-start | bytes 786440 | tf_op jit(solution)/shard_map/while/body/eval_jaxpr/ppermute | solution.py:13
  243.1 10.0 %collective-permute-start = (bf16[64,2048]{1,0:T(8,128)(2,1)}, bf16[64,2048]{1,0:T(8,128)(2,1)S(1)}, u32[]{:S(2)}, u32[]{:S(2)}) collective-permute-start(bf16[64,2048]{1,0:T(8,128)(2,1)} %get-tuple-element.350), channel_id=1, source_target_pairs={{32,0},{64,32},{96,64},{128,96},{160,128},{192,160},{224,192},{256... | collective-permute-start | bytes 786440 | tf_op jit(solution)/shard_map/while/body/eval_jaxpr/ppermute | solution.py:13
  256.9 10.0 %collective-permute-start = (bf16[64,2048]{1,0:T(8,128)(2,1)}, bf16[64,2048]{1,0:T(8,128)(2,1)S(1)}, u32[]{:S(2)}, u32[]{:S(2)}) collective-permute-start(bf16[64,2048]{1,0:T(8,128)(2,1)} %get-tuple-element.350), channel_id=1, source_target_pairs={{32,0},{64,32},{96,64},{128,96},{160,128},{192,160},{224,192},{256... | collective-permute-start | bytes 786440 | tf_op jit(solution)/shard_map/while/body/eval_jaxpr/ppermute | solution.py:13
  270.6 10.0 %collective-permute-start = (bf16[64,2048]{1,0:T(8,128)(2,1)}, bf16[64,2048]{1,0:T(8,128)(2,1)S(1)}, u32[]{:S(2)}, u32[]{:S(2)}) collective-permute-start(bf16[64,2048]{1,0:T(8,128)(2,1)} %get-tuple-element.350), channel_id=1, source_target_pairs={{32,0},{64,32},{96,64},{128,96},{160,128},{192,160},{224,192},{256... | collective-permute-start | bytes 786440 | tf_op jit(solution)/shard_map/while/body/eval_jaxpr/ppermute | solution.py:13
  284.3 10.0 %collective-permute-start = (bf16[64,2048]{1,0:T(8,128)(2,1)}, bf16[64,2048]{1,0:T(8,128)(2,1)S(1)}, u32[]{:S(2)}, u32[]{:S(2)}) collective-permute-start(bf16[64,2048]{1,0:T(8,128)(2,1)} %get-tuple-element.350), channel_id=1, source_target_pairs={{32,0},{64,32},{96,64},{128,96},{160,128},{192,160},{224,192},{256... | collective-permute-start | bytes 786440 | tf_op jit(solution)/shard_map/while/body/eval_jaxpr/ppermute | solution.py:13
  298.1 22.6 %collective-permute-start = (bf16[64,2048]{1,0:T(8,128)(2,1)}, bf16[64,2048]{1,0:T(8,128)(2,1)S(1)}, u32[]{:S(2)}, u32[]{:S(2)}) collective-permute-start(bf16[64,2048]{1,0:T(8,128)(2,1)} %get-tuple-element.350), channel_id=1, source_target_pairs={{32,0},{64,32},{96,64},{128,96},{160,128},{192,160},{224,192},{256... | collective-permute-start | bytes 786440 | tf_op jit(solution)/shard_map/while/body/eval_jaxpr/ppermute | solution.py:13
  330.0 10.0 %collective-permute-start = (bf16[64,2048]{1,0:T(8,128)(2,1)}, bf16[64,2048]{1,0:T(8,128)(2,1)S(1)}, u32[]{:S(2)}, u32[]{:S(2)}) collective-permute-start(bf16[64,2048]{1,0:T(8,128)(2,1)} %get-tuple-element.350), channel_id=1, source_target_pairs={{32,0},{64,32},{96,64},{128,96},{160,128},{192,160},{224,192},{256... | collective-permute-start | bytes 786440 | tf_op jit(solution)/shard_map/while/body/eval_jaxpr/ppermute | solution.py:13
  349.2 6.1 collective-permute-start
  359.1 13.4 %collective-permute-start = (bf16[64,2048]{1,0:T(8,128)(2,1)}, bf16[64,2048]{1,0:T(8,128)(2,1)S(1)}, u32[]{:S(2)}, u32[]{:S(2)}) collective-permute-start(bf16[64,2048]{1,0:T(8,128)(2,1)} %get-tuple-element.350), channel_id=1, source_target_pairs={{32,0},{64,32},{96,64},{128,96},{160,128},{192,160},{224,192},{256... | collective-permute-start | bytes 786440 | tf_op jit(solution)/shard_map/while/body/eval_jaxpr/ppermute | solution.py:13
  376.2 7.9 %collective-permute-start = (bf16[64,2048]{1,0:T(8,128)(2,1)}, bf16[64,2048]{1,0:T(8,128)(2,1)S(1)}, u32[]{:S(2)}, u32[]{:S(2)}) collective-permute-start(bf16[64,2048]{1,0:T(8,128)(2,1)} %get-tuple-element.350), channel_id=1, source_target_pairs={{32,0},{64,32},{96,64},{128,96},{160,128},{192,160},{224,192},{256... | collective-permute-start | bytes 786440 | tf_op jit(solution)/shard_map/while/body/eval_jaxpr/ppermute | solution.py:13
  387.9 7.9 %collective-permute-start = (bf16[64,2048]{1,0:T(8,128)(2,1)}, bf16[64,2048]{1,0:T(8,128)(2,1)S(1)}, u32[]{:S(2)}, u32[]{:S(2)}) collective-permute-start(bf16[64,2048]{1,0:T(8,128)(2,1)} %get-tuple-element.350), channel_id=1, source_target_pairs={{32,0},{64,32},{96,64},{128,96},{160,128},{192,160},{224,192},{256... | collective-permute-start | bytes 786440 | tf_op jit(solution)/shard_map/while/body/eval_jaxpr/ppermute | solution.py:13
  399.5 9.2 %collective-permute-start = (bf16[64,2048]{1,0:T(8,128)(2,1)}, bf16[64,2048]{1,0:T(8,128)(2,1)S(1)}, u32[]{:S(2)}, u32[]{:S(2)}) collective-permute-start(bf16[64,2048]{1,0:T(8,128)(2,1)} %get-tuple-element.350), channel_id=1, source_target_pairs={{32,0},{64,32},{96,64},{128,96},{160,128},{192,160},{224,192},{256... | collective-permute-start | bytes 786440 | tf_op jit(solution)/shard_map/while/body/eval_jaxpr/ppermute | solution.py:13
  412.4 10.0 %collective-permute-start = (bf16[64,2048]{1,0:T(8,128)(2,1)}, bf16[64,2048]{1,0:T(8,128)(2,1)S(1)}, u32[]{:S(2)}, u32[]{:S(2)}) collective-permute-start(bf16[64,2048]{1,0:T(8,128)(2,1)} %get-tuple-element.350), channel_id=1, source_target_pairs={{32,0},{64,32},{96,64},{128,96},{160,128},{192,160},{224,192},{256... | collective-permute-start | bytes 786440 | tf_op jit(solution)/shard_map/while/body/eval_jaxpr/ppermute | solution.py:13
Sparse Core Ops, SparseCore 0:
  11.1 90.6 all-gather.4
  105.0 82.4 all-gather.6
  427.0 232.3 reduce-scatter.1
where the time goes:
time: 669 us; the launch traced here: 667 us
  waiting for transfers between devices  445 us (67%)
  starting transfers between devices  56.1 us (8%)
  local copies, waits for them, and re-layouts  44.6 us (7%)
  other arithmetic  44.6 us (7%)
  blocking collectives  38.7 us (6%)
  between operations  14 us (2%)
  matrix products  13.4 us (2%)
  loops' own time  11 us (2%)
    reduce_scatter x1, waiting for transfers between devices, on_device(): lax.psum_scatter(weight_part.astype(jnp.bfloat16), 'dp', scatter_dimensio...  230 us
    ppermute x16, waiting for transfers between devices, shifted(): return lax.ppermute(x, axis, pairs)  96.2 us
    all_gather x1, waiting for transfers between devices, on_device(): lax.all_gather(up_weight[0], 'dp', axis=0, tiled=True)  85.6 us
    ppermute x16, starting transfers between devices, shifted(): return lax.ppermute(x, axis, pairs)  50.2 us
    all_gather x1, waiting for transfers between devices, on_device(): lax.all_gather(gate_weight[0], 'dp', axis=0, tiled=True)  31.4 us
    dynamic_update_slice x16, other arithmetic, on_device(): lax.scan(one_tick, start_rows, jnp.arange(tick_count - 1, dtype=jnp.int32))  27.8 us
    all_gather x1, blocking collectives, on_device(): seeded = lax.all_gather(cotangent, 'section', axis=1, tiled=True)  21.8 us
    all_to_all x1, blocking collectives, on_device(): lax.all_to_all(blocks, 'section', split_axis=0, concat_axis=0, tiled=True)  16.9 us
  transfers between devices with their start and end apart: 20, of which 19 were waited for; matrix products, arithmetic and copies ran while one was open for 4% of the time, Pallas kernels for 0%

commit v1 on v0

v1 whole, which is shorter than its diff:
```python
import functools

import jax
import jax.numpy as jnp
from jax import lax
from jax.experimental import pallas as pl
from jax.experimental.pallas import tpu as pltpu
from jax.sharding import PartitionSpec as P

NY = 4
ROWS = 64
COLS = 512
F32 = jnp.float32
BF16 = jnp.bfloat16
MESH = pl.DeviceIdType.MESH


def nt_dot(a, b):
    return lax.dot_general(a, b, (((1,), (1,)), ((), ())), preferred_element_type=F32)


def kernel(
    sections,
    nz,
    norm,
    stash,
    cot,
    gate,
    up,
    down,
    gvec,
    gi_out,
    dg_out,
    W,
    x,
    wd,
    g,
    o,
    v,
    acc,
    coef,
    hid,
    hid_t,
    gs,
    part,
    rs,
    ys,
    yr,
    dgv,
    loc_sem,
    agy_s,
    agy_r,
    agz_s,
    agz_r,
    st_s,
    st_r,
    cot_s,
    cot_r,
    ch_s,
    ch_r,
    rs_s,
    rs_r,
    y_s,
    y_r,
):
    last = sections - 1
    half = nz // 2
    tokens, width = x.shape
    ff = wd.shape[0]
    zw = width // nz
    piece = zw // NY
    cw = width // sections
    zr = ff // nz
    yrows = zr // NY
    micro = tokens // ROWS
    chunks = width // COLS
    s = lax.axis_index("section")
    dp = lax.axis_index("dp")
    z = lax.div(dp, NY)
    y = lax.rem(dp, NY)
    dirs = (1, -1)
    offs = (0, 1, 3, 2) if NY == 4 else tuple(range(NY))

    def zmod(a):
        return lax.rem(a + 2 * nz, nz)

    def ymod(a):
        return lax.rem(a + NY, NY)

    def at(zz, yy):
        return zz * NY + yy

    def remote(src, dst, ssem, rsem, **where):
        where = {"section": s, "dp": dp, **where}
        return pltpu.make_async_remote_copy(
            src_ref=src,
            dst_ref=dst,
            send_sem=ssem,
            recv_sem=rsem,
            device_id=(where["section"], where["dp"]),
            device_id_type=MESH,
        )

    def in_half(di, j):
        return (j < NY // 2) == (di == 0)

    own = pl.ds(pl.multiple_of(y * piece, piece), piece)
    loads = [
        pltpu.make_async_copy(gate.at[0], W.at[z, 0, own, :], loc_sem.at[0]),
        pltpu.make_async_copy(up.at[0], W.at[z, 1, own, :], loc_sem.at[1]),
        pltpu.make_async_copy(down.at[0], wd, loc_sem.at[2]),
        pltpu.make_async_copy(gvec, v, loc_sem.at[3]),
    ]
    for load in loads:
        load.start()

    barrier = pltpu.get_barrier_semaphore()

    def greet(section, dpi):
        pl.semaphore_signal(barrier, inc=1, device_id=(section, dpi), device_id_type=MESH)

    for dirn in dirs:
        greet(s, at(zmod(z + dirn), y))
    for off in range(1, NY):
        greet(s, at(z, ymod(y + off)))
    greet(last - s, dp)

    @pl.when(s < last)
    def _():
        greet(s + 1, dp)
        greet(last, dp)

    @pl.when(s > 0)
    def _():
        greet(s - 1, dp)

    @pl.when(s == last)
    def _():
        for other in range(last):
            greet(other, dp)

    @pl.when(s == 0)
    def _():
        pl.semaphore_wait(barrier, NY + 2 + 2)

    @pl.when(jnp.logical_and(s > 0, s < last))
    def _():
        pl.semaphore_wait(barrier, NY + 2 + 3)

    @pl.when(s == last)
    def _():
        pl.semaphore_wait(barrier, NY + 2 + 1 + last)

    def wpiece(zz, yy):
        return W.at[zz, :, pl.ds(pl.multiple_of(yy * piece, piece), piece), :]

    def y_copy(off, src_y):
        return remote(
            wpiece(z, src_y),
            wpiece(z, src_y),
            agy_s.at[off - 1],
            agy_r.at[off - 1],
            dp=at(z, ymod(y + off)),
        )

    def z_copy(di, k, j, zo):
        ref = wpiece(zo, ymod(y + offs[j]))
        return remote(
            ref,
            ref,
            agz_s.at[di, k, j],
            agz_r.at[di, k, j],
            dp=at(zmod(z + dirs[di]), y),
        )

    def z_send(di, k, j):
        return z_copy(di, k, j, zmod(z - dirs[di] * k))

    def z_land(di, k, j):
        return z_copy(di, k, j, zmod(z - dirs[di] * (k + 1)))

    stash_copy = remote(stash.at[0], x, st_s, st_r, section=last - s)
    cot_cols = pl.ds(pl.multiple_of(s * cw, cw), cw)
    cot_copy = remote(cot, g.at[:, cot_cols], cot_s, cot_r.at[s], section=last)
    cot_local = pltpu.make_async_copy(cot, g.at[:, cot_cols], cot_s)

    loads[0].wait()
    loads[1].wait()
    for di in range(2):
        z_send(di, 0, 0).start()
    for off in range(1, NY):
        y_copy(off, y).start()
    stash_copy.start()

    @pl.when(s < last)
    def _():
        cot_copy.start()

    @pl.when(s == last)
    def _():
        cot_local.start()

    acc[...] = jnp.zeros_like(acc)
    loads[3].wait()

    def project(zb):
        cols = x[:, pl.ds(pl.multiple_of(zb * zw, zw), zw)]
        for p in range(2):
            acc[:, p * ff : (p + 1) * ff] += jnp.dot(cols, W[zb, p], preferred_element_type=F32)

    events = sorted(
        ((k, j) for k in range(half + 1) for j in range(NY)), key=lambda e: (e[0] + e[1], -e[0])
    )
    for k, j in events:
        if k == 0:
            if j > 0:
                back = NY - offs[j]
                y_copy(back, ymod(y + offs[j])).wait_recv()
                for di in range(2):
                    z_send(di, 0, j).start()
            if j == NY - 1:
                stash_copy.wait_recv()
                project(z)
        else:
            for di in range(2):
                if k < half or in_half(di, j):
                    z_land(di, k - 1, j).wait_recv()
                    if k < half - 1 or (k == half - 1 and in_half(di, j)):
                        z_send(di, k, j).start()
            if j == NY - 1:
                project(zmod(z - k))
                if k < half:
                    project(zmod(z + k))

    vrow = v[...].astype(F32)
    score = jax.nn.sigmoid(jnp.sum(x[...].astype(F32) * vrow, axis=1, keepdims=True))
    gate_pre = acc[:, :ff]
    up_pre = acc[:, ff:]
    sig = jax.nn.sigmoid(gate_pre)
    act = gate_pre * sig
    hidden = (act * up_pre).astype(BF16).astype(F32)
    coef[:, :ff] = score * up_pre * sig * (1.0 + gate_pre * (1.0 - sig))
    coef[:, ff:] = score * act
    hid[...] = hidden
    hid_t[...] = hidden.T.astype(BF16)
    gs[...] = score
    loads[2].wait()

    def chain_copy(m, c):
        ref = (pl.ds(m * ROWS, ROWS), pl.ds(c * COLS, COLS))
        return remote(
            o.at[ref], g.at[ref], ch_s.at[m, c], ch_r.at[m, c], section=lax.max(s - 1, 0)
        )

    @pl.when(s == last)
    def _():
        cot_local.wait()
        for other in range(last):
            cols = pl.ds(other * cw, cw)
            remote(cot, g.at[:, cols], cot_s, cot_r.at[other], section=last).wait_recv()

    for m in range(micro):
        rows = pl.ds(m * ROWS, ROWS)
        back_proj = jnp.zeros((ROWS, ff), F32)
        for c in range(chunks):
            cols = pl.ds(c * COLS, COLS)

            @pl.when(s < last)
            def _():
                chain_copy(m, c).wait_recv()

            back_proj += nt_dot(g[rows, cols], wd[:, cols])
        gate_grad = (back_proj * coef[rows, :ff]).astype(BF16)
        up_grad = (back_proj * coef[rows, ff:]).astype(BF16)
        row_score = gs[rows, :]
        logit = jnp.sum(back_proj * hid[rows, :], axis=1, keepdims=True)
        logit = logit * row_score * (1.0 - row_score)
        for c in range(chunks):
            for b in range(COLS // zw):
                zb = c * (COLS // zw) + b
                cols = pl.ds(zb * zw, zw)
                through = nt_dot(gate_grad, W[zb, 0]) + nt_dot(up_grad, W[zb, 1])
                total = g[rows, cols].astype(F32) + through
                total = total + logit * v[:, cols].astype(F32)
                o[rows, cols] = total.astype(BF16)

            @pl.when(s > 0)
            def _():
                chain_copy(m, c).start()

    gi_copy = pltpu.make_async_copy(o, gi_out, loc_sem.at[0])
    gi_copy.start()

    x[...] = (gs[...] * g[...].astype(F32)).astype(BF16)

    def block(zz):
        start = pl.multiple_of(zz * zr, zr)
        rows = pl.ds(start, zr)
        part[rows, :] = jnp.dot(hid_t[rows, :], x[...], preferred_element_type=F32).astype(BF16)

    def sub(zz, j):
        return pl.ds(pl.multiple_of(zz * zr + ymod(y + offs[j]) * yrows, yrows), yrows)

    def lane(j):
        return pl.ds(pl.multiple_of(ymod(y + offs[j]) * yrows, yrows), yrows)

    def rs_copy(di, d, j):
        return remote(
            part.at[sub(zmod(z + dirs[di] * d), j), :],
            rs.at[di, d - 1, lane(j), :],
            rs_s.at[di, d - 1, j],
            rs_r.at[di, d - 1, j],
            dp=at(zmod(z + dirs[di]), y),
        )

    order = tuple(range(NY - 1, -1, -1))
    block(zmod(z + half))
    for j in order:
        for di in range(2):
            if in_half(di, j):
                rs_copy(di, half, j).start()
    for d in range(half - 1, 0, -1):
        for di in range(2):
            block(zmod(z + dirs[di] * d))
        for di in range(2):
            js = order
            if d == half - 1:
                js = [j for j in order if not in_half(di, j)] + [j for j in order if in_half(di, j)]
            for j in js:
                if d < half - 1 or in_half(di, j):
                    rs_copy(di, d + 1, j).wait_recv()
                    rows = sub(zmod(z + dirs[di] * d), j)
                    total = part[rows, :].astype(F32) + rs[di, d, lane(j), :].astype(F32)
                    part[rows, :] = total.astype(BF16)
                rs_copy(di, d, j).start()
    block(z)

    def y_sum_copy(off):
        return remote(
            ys.at[off - 1], yr.at[off - 1], y_s.at[off - 1], y_r.at[off - 1], dp=at(z, ymod(y + off))
        )

    for j in order:
        total = part[sub(z, j), :].astype(F32)
        for di in range(2):
            rs_copy(di, 1, j).wait_recv()
            total = total + rs[di, 0, lane(j), :].astype(F32)
        if offs[j] == 0:
            dgv[...] = total
        else:
            ys[offs[j] - 1] = total.astype(BF16)
            y_sum_copy(offs[j]).start()
    total = dgv[...]
    for off in range(1, NY):
        y_sum_copy(off).wait_recv()
        total = total + yr[off - 1].astype(F32)
    dgv[...] = total * norm
    dg_copy = pltpu.make_async_copy(dgv, dg_out, loc_sem.at[1])
    dg_copy.start()

    for off in range(1, NY):
        y_copy(off, y).wait_send()
        y_sum_copy(off).wait_send()
    for di in range(2):
        for j in range(NY):
            for k in range(half):
                if k < half - 1 or in_half(di, j):
                    z_send(di, k, j).wait_send()
                    rs_copy(di, k + 1, j).wait_send()
    stash_copy.wait_send()

    @pl.when(s < last)
    def _():
        cot_copy.wait_send()

    @pl.when(s > 0)
    def _():
        for m in range(micro):
            for c in range(chunks):
                chain_copy(m, c).wait_send()

    gi_copy.wait()
    dg_copy.wait()


def on_device(sections, nz, stash, cotangent, gate_weight, up_weight, down_weight, shared_gate):
    tokens, width = stash.shape[1:]
    ff = down_weight.shape[1]
    half = nz // 2
    zr = ff // nz
    yrows = zr // NY
    micro = tokens // ROWS
    chunks = width // COLS
    norm = (tokens * nz * NY) ** (-0.5)
    dma = pltpu.SemaphoreType.DMA
    hbm = pl.BlockSpec(memory_space=pl.ANY)
    results, grad = pl.pallas_call(
        functools.partial(kernel, sections, nz, norm),
        out_shape=(
            jax.ShapeDtypeStruct((tokens, width), BF16),
            jax.ShapeDtypeStruct((yrows, width), F32),
        ),
        in_specs=[hbm] * 6,
        out_specs=(hbm, hbm),
        scratch_shapes=[
            pltpu.VMEM((nz, 2, width // nz, ff), BF16),
            pltpu.VMEM((tokens, width), BF16),
            pltpu.VMEM((ff, width), BF16),
            pltpu.VMEM((tokens, width), BF16),
            pltpu.VMEM((tokens, width), BF16),
            pltpu.VMEM((1, width), BF16),
            pltpu.VMEM((tokens, 2 * ff), F32),
            pltpu.VMEM((tokens, 2 * ff), F32),
            pltpu.VMEM((tokens, ff), F32),
            pltpu.VMEM((ff, tokens), BF16),
            pltpu.VMEM((tokens, 1), F32),
            pltpu.VMEM((ff, width), BF16),
            pltpu.VMEM((2, half, zr, width), BF16),
            pltpu.VMEM((NY - 1, yrows, width), BF16),
            pltpu.VMEM((NY - 1, yrows, width), BF16),
            pltpu.VMEM((yrows, width), F32),
            dma((4,)),
            dma((NY - 1,)),
            dma((NY - 1,)),
            dma((2, half, NY)),
            dma((2, half, NY)),
            dma,
            dma,
            dma,
            dma((sections,)),
            dma((micro, chunks)),
            dma((micro, chunks)),
            dma((2, half, NY)),
            dma((2, half, NY)),
            dma((NY - 1,)),
            dma((NY - 1,)),
        ],
        compiler_params=pltpu.CompilerParams(
            collective_id=0, has_side_effects=True, vmem_limit_bytes=48 * 2**20
        ),
        name="chain",
    )(stash, cotangent, gate_weight, up_weight, down_weight, shared_gate)
    return results[None], grad[None]


def solution(mesh):
    placed = (
        P("section", "dp", None),
        P("dp", "section"),
        P("section", "dp", None),
        P("section", "dp", None),
        P("section", None, None),
        P("section", None),
    )
    return jax.shard_map(
        functools.partial(on_device, mesh.shape["section"], mesh.shape["dp"] // NY),
        mesh=mesh,
        in_specs=placed,
        out_specs=(P("section", "dp", None), P("section", "dp", None)),
        check_vma=False,
    )
```

time: 669 us -> 173 us (0.26)
  the two profiles are of different devices: /device:TPU:6 before, /device:TPU:64 now
where the time goes in v1:
time: 173 us; the launch traced here: 172 us
  Pallas kernels  165 us (95%)
  local copies, waits for them, and re-layouts  7.21 us (4%)
    pallas_call x1, Pallas kernels, on_device(): pl.pallas_call(functools.partial(kernel, sections, nz, norm), out_shape=(...  165 us
    unnamed x14, local copies, waits for them, and re-layouts  7.21 us

profile of v1, /device:TPU:64, one launch (start us, length us, event | category | flops | bytes accessed | tf_op | source)
XLA Modules:
  0.0 172.4 jit_solution(3540021921165102870)
XLA Ops:
  0.6 0.0 copy-start
  0.6 1.6 copy-done
  2.2 0.0 copy-start.1
  2.2 1.0 copy-done.1
  3.3 0.0 copy-start.2
  3.3 0.8 copy-done.2
  4.1 0.0 copy-start.3
  4.1 0.8 copy-done.3
  4.9 0.0 copy-start.4
  4.9 0.8 copy-done.4
  5.7 0.0 copy-start.5
  5.7 0.7 copy-done.5
  6.4 164.5 %chain.1 = (bf16[128,2048]{1,0:T(8,128)(2,1)S(1)}, f32[16,2048]{1,0:T(8,128)S(1)}) custom-call(bf16[1,128,2048]{2,1,0:T(8,128)(2,1)S(1)} %copy-done.1, bf16[128,128]{1,0:T(8,128)(2,1)S(1)} %copy-done.4, bf16[1,64,512]{2,1,0:T(8,128)(2,1)S(1)} %copy-done.2, bf16[1,64,512]{2,1,0:T(8,128)(2,1)S(1)} %copy-done.3, bf16[1,512,2048]{2,1,0:T(8,128)(2,1)S(1)} %copy-done, ...), custom_call_target="tpu_custom_call" | custom-call | tf_op jit(solution)/shard_map/chain/pallas_call | solution.py:397
  171.0 0.8 copy.10
  171.8 0.7 copy.11
Async XLA Ops:
  0.6 1.6 copy-start
  2.2 1.0 copy-start.1
  3.3 0.8 copy-start.2
  4.1 0.8 copy-start.3
  4.9 0.8 copy-start.4
  5.7 0.7 copy-start.5
